TPU v7x, 32 devices: a whole 2x2x4 slice. The times are simulated.
32 devices in a mesh: energy: 8 (over y, x, core), elem: 4 (over z).
Axes of the slice: x: 2, y: 2, z: 4, core: 2. Of those that a mesh axis runs over, the one named last changes fastest.
Arguments:
- g_lesser: bfloat16 [2, 512, 2048], P(None, 'energy', 'elem'), may hold values from -6 to 6
- g_greater: bfloat16 [2, 512, 2048], P(None, 'energy', 'elem'), may hold values from -6 to 6
- send_rows: int32 [4, 8, 4, 32], P('elem'), may hold values from 0 to 63, as said below
- partner_slot: int32 [2048], P('elem'), may hold values from 0 to 127, as said below
Outputs:
- polarization_lesser: bfloat16 [2, 512, 2048], P(None, 'energy', 'elem')
- polarization_greater: bfloat16 [2, 512, 2048], P(None, 'energy', 'elem')
Inputs may be any that keep to these rules, and one draw needn't show every extreme that they name: partner is an involution on the elements that keeps the element piece n. The groups fall into two halves of 2 groups; for a sending group b and element piece n, send_rows[b, n, a, :] lists 32 distinct rows when a lies in b's half (b itself included) and zeros otherwise; every row of that piece of the sender appears exactly once over all receivers of its half. `partner_slot`: every slot named points into a receiving group's half and to a slot that carries a row; the 64 elements of one element piece of a group name 64 distinct slots.
All inputs are finite; a program needn't handle non-finite values.
Results may differ from a plain program's by a relative error of at most 0.001.
Values may be sent and summed in bfloat16 or wider, within the bound.
No kernel may reach another device: no remote copies, remote signals or barrier semaphores. Data moves between devices by JAX's collectives and lax.ppermute only.
A program may use at most 64 MiB of HBM per device.

v0:
```python
from functools import partial
import math
import jax
import jax.numpy as jnp
from jax import lax
from jax.sharding import PartitionSpec as P


def factor_pair(length):
    divisor = math.isqrt(length)
    while length % divisor:
        divisor -= 1
    return divisor


def phase_tables(rows_count, cols_count, modulus, inverse):
    sign_factor = 1.0 if inverse else -1.0
    left_index = jnp.arange(rows_count, dtype=jnp.int32)
    right_index = jnp.arange(cols_count, dtype=jnp.int32)
    phases = (left_index[:, None] * right_index[None, :] % modulus).astype(jnp.float32) * (
        2.0 * math.pi / modulus
    )
    return (jnp.cos(phases), sign_factor * jnp.sin(phases))


def transform(real_part, imag_part, inverse):
    signals, length, width = real_part.shape
    first_size = factor_pair(length)
    second_size = length // first_size
    cos_first, sin_first = phase_tables(first_size, first_size, first_size, inverse)
    cos_twist, sin_twist = phase_tables(first_size, second_size, length, inverse)
    cos_second, sin_second = phase_tables(second_size, second_size, second_size, inverse)
    product = partial(jnp.einsum, precision=lax.Precision.HIGHEST)
    real_grid = real_part.reshape(signals, first_size, second_size, width)
    imag_grid = imag_part.reshape(signals, first_size, second_size, width)
    inner_re = product("ka,sabe->skbe", cos_first, real_grid) - product(
        "ka,sabe->skbe", sin_first, imag_grid
    )
    inner_im = product("ka,sabe->skbe", cos_first, imag_grid) + product(
        "ka,sabe->skbe", sin_first, real_grid
    )
    twist_cos = cos_twist[None, :, :, None]
    twist_sin = sin_twist[None, :, :, None]
    twist_re = inner_re * twist_cos - inner_im * twist_sin
    twist_im = inner_re * twist_sin + inner_im * twist_cos
    outer_re = product("qb,skbe->sqke", cos_second, twist_re) - product(
        "qb,skbe->sqke", sin_second, twist_im
    )
    outer_im = product("qb,skbe->sqke", cos_second, twist_im) + product(
        "qb,skbe->sqke", sin_second, twist_re
    )
    return (outer_re.reshape(signals, length, width), outer_im.reshape(signals, length, width))


def reverse_energy(values):
    return jnp.roll(jnp.flip(values, axis=1), 1, axis=1)


def shards(g_lesser, g_greater, send_rows, partner_slot):
    piece_index = lax.axis_index("energy")
    energy_count = lax.axis_size("energy")
    group_rows = partner_slot.shape[0]
    elem_dev = group_rows // energy_count
    own_lesser, own_greater = (
        lax.all_to_all(g_lesser, "energy", split_axis=2, concat_axis=1, tiled=True),
        lax.all_to_all(g_greater, "energy", split_axis=2, concat_axis=1, tiled=True),
    )
    own_rows = jnp.stack([own_lesser, own_greater])
    partner_columns = lax.dynamic_slice_in_dim(partner_slot, piece_index * elem_dev, elem_dev, 0)
    chosen_rows = lax.dynamic_index_in_dim(send_rows[0], piece_index, 0, keepdims=False).reshape(-1)
    outgoing = jnp.take(own_rows, chosen_rows, axis=3)
    incoming = lax.all_to_all(outgoing, "elem", split_axis=3, concat_axis=3, tiled=True)
    partner_rows = jnp.take(incoming, partner_columns, axis=3)
    signals = jnp.concatenate([own_rows, partner_rows], 0).astype(jnp.float32)
    spec_re, spec_im = transform(signals[:, 0], signals[:, 1], False)
    near_re = spec_re[:2]
    near_im = spec_im[:2]
    far_re = reverse_energy(jnp.stack([spec_re[3], spec_re[2]]))
    far_im = reverse_energy(jnp.stack([spec_im[3], spec_im[2]]))
    prod_re = near_re * far_re - near_im * far_im
    prod_im = near_re * far_im + near_im * far_re
    back_re, back_im = transform(prod_re, prod_im, True)
    length = back_re.shape[1]
    factor = 1.0 / (length * math.sqrt(length))
    result = jnp.stack([factor * back_im, -factor * back_re], 1).astype(jnp.bfloat16)
    lesser_out, greater_out = (
        lax.all_to_all(result[0], "energy", split_axis=1, concat_axis=2, tiled=True),
        lax.all_to_all(result[1], "energy", split_axis=1, concat_axis=2, tiled=True),
    )
    return (lesser_out, greater_out)


def solution(mesh):
    in_specs = (
        P(None, "energy", "elem"),
        P(None, "energy", "elem"),
        P("elem", None, None, None),
        P("elem"),
    )
    out_specs = (P(None, "energy", "elem"), P(None, "energy", "elem"))
    return jax.shard_map(shards, mesh=mesh, in_specs=in_specs, out_specs=out_specs, check_vma=False)
```

profile of v0, /device:TPU:0, one launch (start us, length us, event | category | flops | bytes accessed | tf_op | source)
XLA Modules:
  0.0 93.1 jit_solution(4972418240594326676)
XLA Ops:
  0.6 1.1 %copy.86 = bf16[2,64,512]{1,0,2:T(2,128)(2,1)S(1)} copy(bf16[2,64,512]{2,1,0:T(8,128)(2,1)} %param.4) | data formatting | bytes 262144 | tf_op args[0]
  1.7 0.9 reshape.175
  2.6 5.3 %all-to-all-start = ((bf16[8,2,4096]{2,1,0:T(2,128)(2,1)}), bf16[8,2,4096]{2,1,0:T(2,128)(2,1)S(1)}, u32[]{:S(2)}, u32[]{:S(2)}) async-start(bf16[8,2,4096]{2,1,0:T(2,128)(2,1)} %reshape.175), calls=%async_computation | async-start | bytes 262144 | tf_op jit(solution)/shard_map/all_to_all | solution.py:65
  8.3 0.9 reshape.173
  9.2 4.3 %all-to-all-done = bf16[8,2,4096]{2,1,0:T(2,128)(2,1)S(1)} async-done(((bf16[8,2,4096]{2,1,0:T(2,128)(2,1)}), bf16[8,2,4096]{2,1,0:T(2,128)(2,1)S(1)}, u32[]{:S(2)}, u32[]{:S(2)}) %all-to-all-start) | async-done | bytes 131104 | tf_op jit(solution)/shard_map/all_to_all | solution.py:65
  13.5 3.4 %all-to-all-start.1 = ((bf16[8,2,4096]{2,1,0:T(2,128)(2,1)}), bf16[8,2,4096]{2,1,0:T(2,128)(2,1)S(1)}, u32[]{:S(2)}, u32[]{:S(2)}) async-start(bf16[8,2,4096]{2,1,0:T(2,128)(2,1)} %reshape.173), calls=%async_computation.1 | async-start | bytes 262144 | tf_op jit(solution)/shard_map/all_to_all | solution.py:66
  17.6 4.7 %all-to-all-done.1 = bf16[8,2,4096]{2,1,0:T(2,128)(2,1)S(1)} async-done(((bf16[8,2,4096]{2,1,0:T(2,128)(2,1)}), bf16[8,2,4096]{2,1,0:T(2,128)(2,1)S(1)}, u32[]{:S(2)}, u32[]{:S(2)}) %all-to-all-start.1) | async-done | bytes 131104 | tf_op jit(solution)/shard_map/all_to_all | solution.py:66
  23.4 1.7 %gather_fusion = bf16[128,2,2,512]{3,2,1,0:T(2,128)(2,1)S(1)} fusion(bf16[2,2,512,64]{2,1,3,0:T(2,128)(2,1)S(1)} %pad_maximum_fusion.4, s32[1024]{0:T(1024)S(1)} %pad_clamp_fusion.1), kind=kCustom, calls=%fused_computation | custom fusion | bytes 1049088 | tf_op jit(solution)/shard_map/jit(_take)/gather | solution.py:71
  25.1 1.4 %fusion.22 = bf16[2,2,512,128]{2,1,0,3:T(2,128)(2,1)} fusion(bf16[128,2,2,512]{3,2,1,0:T(2,128)(2,1)S(1)} %gather_fusion, pred[128]{0:T(512)(128)(4,1)S(1)} %compare_and_fusion), kind=kLoop, calls=%fused_computation.49 | loop fusion | flops 262144 | bytes 1048704 | tf_op jit(solution)/shard_map/jit(_take)/select_n | solution.py:71
  26.5 4.9 %all-to-all-start.2 = ((bf16[2,2,512,128]{2,1,0,3:T(2,128)(2,1)}), bf16[2,2,512,128]{2,1,0,3:T(2,128)(2,1)S(1)}, u32[]{:S(2)}, u32[]{:S(2)}) async-start(bf16[2,2,512,128]{2,1,0,3:T(2,128)(2,1)} %fusion.22), calls=%async_computation.2 | async-start | bytes 1048576 | tf_op jit(solution)/shard_map/all_to_all | solution.py:72
  32.6 13.1 %all-to-all-done.2 = bf16[2,2,512,128]{2,1,0,3:T(2,128)(2,1)S(1)} async-done(((bf16[2,2,512,128]{2,1,0,3:T(2,128)(2,1)}), bf16[2,2,512,128]{2,1,0,3:T(2,128)(2,1)S(1)}, u32[]{:S(2)}, u32[]{:S(2)}) %all-to-all-start.2) | async-done | bytes 524320 | tf_op jit(solution)/shard_map/all_to_all | solution.py:72
  46.0 1.1 %gather_fusion.1 = bf16[64,2,2,512]{3,2,1,0:T(2,128)(2,1)S(1)} fusion(bf16[2,2,512,128]{2,1,3,0:T(2,128)(2,1)S(1)} %copy.92, s32[1024]{0:T(1024)S(1)} %pad_clamp_fusion), kind=kCustom, calls=%fused_computation.1 | custom fusion | bytes 524544 | tf_op jit(solution)/shard_map/jit(_take)/gather | solution.py:73
  53.0 1.4 %fusion.12 = f32[4,16,64,32]{2,3,1,0:T(8,128)S(1)} fusion(f32[4,16,32,64]{3,1,2,0:T(8,128)S(1)} %get-tuple-element.4), kind=kOutput, calls=%fused_computation.25 | convolution fusion | flops 50345984 | bytes 1048576 | tf_op jit(solution)/shard_map/qb,skbe->sqke/dot_general | solution.py:49
  54.4 1.4 %fusion.16 = f32[4,16,64,32]{2,3,1,0:T(8,128)S(1)} fusion(f32[4,16,32,64]{3,1,2,0:T(8,128)S(1)} %get-tuple-element.5), kind=kOutput, calls=%fused_computation.29 | convolution fusion | flops 50345984 | bytes 1048576 | tf_op jit(solution)/shard_map/qb,skbe->sqke/dot_general | solution.py:46
  55.8 1.4 %fusion.1 = f32[4,32,16,64]{3,1,2,0:T(8,128)S(1)} fusion(f32[4,16,64,32]{2,3,1,0:T(8,128)S(1)} %fusion.16, f32[4,16,32,64]{3,1,2,0:T(8,128)S(1)} %get-tuple-element.4), kind=kOutput, calls=%fused_computation.5 | convolution fusion | flops 50478080 | bytes 1572864 | tf_op jit(solution)/shard_map/qb,skbe->sqke/dot_general | solution.py:46
  57.2 1.0 %copy-done.1 = f32[4,32,16,64]{3,1,2,0:T(8,128)} copy-done((f32[4,32,16,64]{3,1,2,0:T(8,128)}, f32[4,32,16,64]{3,1,2,0:T(8,128)S(1)}, u32[]{:S(2)}) %copy-start.1) | copy-done | bytes 524312
  58.2 1.4 %fusion = f32[4,32,16,64]{3,1,2,0:T(8,128)S(1)} fusion(f32[4,16,64,32]{2,3,1,0:T(8,128)S(1)} %fusion.12, f32[4,16,32,64]{3,1,2,0:T(8,128)S(1)} %get-tuple-element.5), kind=kOutput, calls=%fused_computation.3 | convolution fusion | flops 50478080 | bytes 1572864 | tf_op jit(solution)/shard_map/qb,skbe->sqke/dot_general | solution.py:49
  59.6 1.0 %copy-done.2 = f32[4,32,16,64]{3,1,2,0:T(8,128)} copy-done((f32[4,32,16,64]{3,1,2,0:T(8,128)}, f32[4,32,16,64]{3,1,2,0:T(8,128)S(1)}, u32[]{:S(2)}) %copy-start.2) | copy-done | bytes 524312
  67.5 0.9 fusion.7
  68.4 1.1 %multiply_subtract_fusion.1 = (f32[2,16,32,64]{3,1,2,0:T(8,128)S(1)}, f32[2,16,32,64]{3,1,2,0:T(8,128)S(1)}) fusion(f32[2,16,32,64]{3,1,2,0:T(8,128)S(1)} %fusion.7, f32[16,32]{0,1:T(8,128)S(1)} %get-tuple-element.19, f32[16,32]{0,1:T(8,128)S(1)} %fusion.90, f32[2,32,64,16]{2,3,1,0:T(8,128)S(1)} %fusion.29, f32[2,16,32,64]{3,2,1,0:T(8,128)S(1)} %get-tuple-element.6), kind=kOutput, calls=%fused_computation.47 | convolution fusion | flops 13045248 | bytes 1314816 | tf_op jit(solution)/shard_map/ka,sabe->skbe/dot_general | solution.py:39
  74.1 3.4 %all-to-all-start.4 = ((bf16[8,2,4096]{2,1,0:T(2,128)(2,1)}), bf16[8,2,4096]{2,1,0:T(2,128)(2,1)S(1)}, u32[]{:S(2)}, u32[]{:S(2)}) async-start(bf16[8,2,4096]{2,1,0:T(2,128)(2,1)} %reshape.179), calls=%async_computation.4 | async-start | bytes 262144 | tf_op jit(solution)/shard_map/all_to_all | solution.py:88
  78.7 4.3 %all-to-all-done.4 = bf16[8,2,4096]{2,1,0:T(2,128)(2,1)S(1)} async-done(((bf16[8,2,4096]{2,1,0:T(2,128)(2,1)}), bf16[8,2,4096]{2,1,0:T(2,128)(2,1)S(1)}, u32[]{:S(2)}, u32[]{:S(2)}) %all-to-all-start.4) | async-done | bytes 131104 | tf_op jit(solution)/shard_map/all_to_all | solution.py:88
  83.0 3.4 %all-to-all-start.3 = ((bf16[8,2,4096]{2,1,0:T(2,128)(2,1)}), bf16[8,2,4096]{2,1,0:T(2,128)(2,1)S(1)}, u32[]{:S(2)}, u32[]{:S(2)}) async-start(bf16[8,2,4096]{2,1,0:T(2,128)(2,1)} %reshape.177), calls=%async_computation.3 | async-start | bytes 262144 | tf_op jit(solution)/shard_map/all_to_all | solution.py:87
  87.6 4.2 %all-to-all-done.3 = bf16[8,2,4096]{2,1,0:T(2,128)(2,1)S(1)} async-done(((bf16[8,2,4096]{2,1,0:T(2,128)(2,1)}), bf16[8,2,4096]{2,1,0:T(2,128)(2,1)S(1)}, u32[]{:S(2)}, u32[]{:S(2)}) %all-to-all-start.3) | async-done | bytes 131104 | tf_op jit(solution)/shard_map/all_to_all | solution.py:87
  (76 shorter events, 24.7 us)
Async XLA Ops:
  0.6 7.3 %copy-start = (s32[1,8,4,32]{3,2,1,0:T(4,128)S(1)}, s32[1,8,4,32]{3,2,1,0:T(4,128)}, u32[]{:S(2)}) copy-start(s32[1,8,4,32]{3,2,1,0:T(4,128)} %param.6) | copy-start | bytes 12292
  2.6 5.5 %copy-start.3 = (bf16[2,64,512]{2,1,0:T(8,128)(2,1)S(1)}, bf16[2,64,512]{2,1,0:T(8,128)(2,1)}, u32[]{:S(2)}) copy-start(bf16[2,64,512]{2,1,0:T(8,128)(2,1)} %param.5) | copy-start | bytes 393220
  2.6 10.8 %all-to-all-start = ((bf16[8,2,4096]{2,1,0:T(2,128)(2,1)}), bf16[8,2,4096]{2,1,0:T(2,128)(2,1)S(1)}, u32[]{:S(2)}, u32[]{:S(2)}) async-start(bf16[8,2,4096]{2,1,0:T(2,128)(2,1)} %reshape.175), calls=%async_computation | async-start | bytes 262144 | tf_op jit(solution)/shard_map/all_to_all | solution.py:65
  13.5 8.8 %all-to-all-start.1 = ((bf16[8,2,4096]{2,1,0:T(2,128)(2,1)}), bf16[8,2,4096]{2,1,0:T(2,128)(2,1)S(1)}, u32[]{:S(2)}, u32[]{:S(2)}) async-start(bf16[8,2,4096]{2,1,0:T(2,128)(2,1)} %reshape.173), calls=%async_computation.1 | async-start | bytes 262144 | tf_op jit(solution)/shard_map/all_to_all | solution.py:66
  26.5 19.2 %all-to-all-start.2 = ((bf16[2,2,512,128]{2,1,0,3:T(2,128)(2,1)}), bf16[2,2,512,128]{2,1,0,3:T(2,128)(2,1)S(1)}, u32[]{:S(2)}, u32[]{:S(2)}) async-start(bf16[2,2,512,128]{2,1,0,3:T(2,128)(2,1)} %fusion.22), calls=%async_computation.2 | async-start | bytes 1048576 | tf_op jit(solution)/shard_map/all_to_all | solution.py:72
  57.2 1.0 %copy-start.1 = (f32[4,32,16,64]{3,1,2,0:T(8,128)}, f32[4,32,16,64]{3,1,2,0:T(8,128)S(1)}, u32[]{:S(2)}) copy-start(f32[4,32,16,64]{3,1,2,0:T(8,128)S(1)} %fusion.1) | copy-start | bytes 1572868
  59.6 1.0 %copy-start.2 = (f32[4,32,16,64]{3,1,2,0:T(8,128)}, f32[4,32,16,64]{3,1,2,0:T(8,128)S(1)}, u32[]{:S(2)}) copy-start(f32[4,32,16,64]{3,1,2,0:T(8,128)S(1)} %fusion) | copy-start | bytes 1572868
  60.6 1.0 %slice-start = ((f32[4,32,16,64]{3,1,2,0:T(8,128)}), f32[2,32,16,64]{3,1,2,0:T(8,128)S(1)}, s32[]{:S(2)}) async-start(f32[4,32,16,64]{3,1,2,0:T(8,128)} %copy-done.1), calls=%async_computation.5 | async-start | bytes 1048576 | tf_op jit(solution)/shard_map/slice | solution.py:76
  62.9 1.0 %slice-start.1 = ((f32[4,32,16,64]{3,1,2,0:T(8,128)}), f32[2,32,16,64]{3,1,2,0:T(8,128)S(1)}, s32[]{:S(2)}) async-start(f32[4,32,16,64]{3,1,2,0:T(8,128)} %copy-done.2), calls=%async_computation.6 | async-start | bytes 1048576 | tf_op jit(solution)/shard_map/slice | solution.py:77
  74.1 8.8 %all-to-all-start.4 = ((bf16[8,2,4096]{2,1,0:T(2,128)(2,1)}), bf16[8,2,4096]{2,1,0:T(2,128)(2,1)S(1)}, u32[]{:S(2)}, u32[]{:S(2)}) async-start(bf16[8,2,4096]{2,1,0:T(2,128)(2,1)} %reshape.179), calls=%async_computation.4 | async-start | bytes 262144 | tf_op jit(solution)/shard_map/all_to_all | solution.py:88
  83.0 8.8 %all-to-all-start.3 = ((bf16[8,2,4096]{2,1,0:T(2,128)(2,1)}), bf16[8,2,4096]{2,1,0:T(2,128)(2,1)S(1)}, u32[]{:S(2)}, u32[]{:S(2)}) async-start(bf16[8,2,4096]{2,1,0:T(2,128)(2,1)} %reshape.177), calls=%async_computation.3 | async-start | bytes 262144 | tf_op jit(solution)/shard_map/all_to_all | solution.py:87
where the time goes:
time: 93.8 us; the launch traced here: 93.1 us
  waiting for transfers between devices  30.5 us (33%)
  local copies, waits for them, and re-layouts  21.7 us (23%)
  starting transfers between devices  20.3 us (22%)
  matrix products  15.2 us (16%)
  other arithmetic  4.33 us (5%)
  between operations  1.15 us (1%)
    all_to_all x1, waiting for transfers between devices, shards(): lax.all_to_all(outgoing, 'elem', split_axis=3, concat_axis=3, tiled=True)  13.1 us
    unnamed x18, local copies, waits for them, and re-layouts  7.64 us
    all_to_all x1, starting transfers between devices, shards(): lax.all_to_all(g_lesser, 'energy', split_axis=2, concat_axis=1, tiled=True)  5.3 us
    all_to_all x1, starting transfers between devices, shards(): lax.all_to_all(outgoing, 'elem', split_axis=3, concat_axis=3, tiled=True)  4.87 us
    all_to_all x1, waiting for transfers between devices, shards(): lax.all_to_all(g_greater, 'energy', split_axis=2, concat_axis=1, tiled=True)  4.68 us
    all_to_all x1, waiting for transfers between devices, shards(): lax.all_to_all(result[1], 'energy', split_axis=1, concat_axis=2, tiled=True)  4.29 us
    all_to_all x1, waiting for transfers between devices, shards(): lax.all_to_all(g_lesser, 'energy', split_axis=2, concat_axis=1, tiled=True)  4.26 us
    all_to_all x1, waiting for transfers between devices, shards(): lax.all_to_all(result[0], 'energy', split_axis=1, concat_axis=2, tiled=True)  4.19 us
  transfers between devices with their start and end apart: 5, of which 5 were waited for; matrix products, arithmetic and copies ran while one was open for 5% of the time, Pallas kernels for 0%

commit v1 on v0

--- a/solution.py
+++ b/solution.py
@@ -85,7 +85,12 @@
     result = jnp.stack([factor * back_im, -factor * back_re], 1).astype(jnp.bfloat16)
     lesser_out, greater_out = (
         lax.all_to_all(result[0], "energy", split_axis=1, concat_axis=2, tiled=True),
-        lax.all_to_all(result[1], "energy", split_axis=1, concat_axis=2, tiled=True),
+        jnp.concatenate(
+            lax.all_to_all(
+                jnp.stack(jnp.split(result[1], lax.axis_size("energy"), axis=1)), "energy", 0, 0
+            ),
+            axis=2,
+        ),
     )
     return (lesser_out, greater_out)
 

time: 93.8 us -> 93.8 us (level)
    reshape x0 -> x2, local copies, waits for them, and re-layouts: none -> 1.04 us  [shards(): jnp.concatenate(lax.all_to_all(jnp.stack(jnp.split(result[1], lax.axis_si...]
    all_to_all x2 -> x0, local copies, waits for them, and re-layouts: 1.04 us -> none  [shards(): lax.all_to_all(result[1], 'energy', split_axis=1, concat_axis=2, tiled=True)]
    unnamed x18 -> x25, local copies, waits for them, and re-layouts: 7.64 us -> 7.71 us
where the time goes in v1:
time: 93.8 us; the launch traced here: 93.1 us
  waiting for transfers between devices  30.6 us (33%)
  local copies, waits for them, and re-layouts  21.5 us (23%)
  starting transfers between devices  20.3 us (22%)
  matrix products  15.2 us (16%)
  other arithmetic  4.33 us (5%)
  between operations  1.19 us (1%)
    all_to_all x1, waiting for transfers between devices, shards(): lax.all_to_all(outgoing, 'elem', split_axis=3, concat_axis=3, tiled=True)  13.1 us
    unnamed x25, local copies, waits for them, and re-layouts  7.71 us
    all_to_all x1, starting transfers between devices, shards(): lax.all_to_all(g_lesser, 'energy', split_axis=2, concat_axis=1, tiled=True)  5.3 us
    all_to_all x1, starting transfers between devices, shards(): lax.all_to_all(outgoing, 'elem', split_axis=3, concat_axis=3, tiled=True)  4.87 us
    all_to_all x1, waiting for transfers between devices, shards(): lax.all_to_all(g_greater, 'energy', split_axis=2, concat_axis=1, tiled=True)  4.68 us
    all_to_all x1, waiting for transfers between devices, shards(): lax.all_to_all(result[0], 'energy', split_axis=1, concat_axis=2, tiled=True)  4.45 us
    all_to_all x1, waiting for transfers between devices, shards(): lax.all_to_all(g_lesser, 'energy', split_axis=2, concat_axis=1, tiled=True)  4.26 us
    all_to_all x1, waiting for transfers between devices, shards(): lax.all_to_all(jnp.stack(jnp.split(result[1], lax.axis_size('energy'), ax...  4.19 us
  transfers between devices with their start and end apart: 5, of which 5 were waited for; matrix products, arithmetic and copies ran while one was open for 5% of the time, Pallas kernels for 0%

profile of v1, /device:TPU:0, one launch (start us, length us, event | category | flops | bytes accessed | tf_op | source)
XLA Modules:
  0.0 93.1 jit_solution(12157943108908006727)
XLA Ops:
  0.6 1.1 %copy.91 = bf16[2,64,512]{1,0,2:T(2,128)(2,1)S(1)} copy(bf16[2,64,512]{2,1,0:T(8,128)(2,1)} %param.4) | data formatting | bytes 262144 | tf_op args[0]
  1.7 0.9 reshape.183
  2.6 5.3 %all-to-all-start = ((bf16[8,2,4096]{2,1,0:T(2,128)(2,1)}), bf16[8,2,4096]{2,1,0:T(2,128)(2,1)S(1)}, u32[]{:S(2)}, u32[]{:S(2)}) async-start(bf16[8,2,4096]{2,1,0:T(2,128)(2,1)} %reshape.183), calls=%async_computation | async-start | bytes 262144 | tf_op jit(solution)/shard_map/all_to_all | solution.py:65
  8.3 0.9 reshape.181
  9.2 4.3 %all-to-all-done = bf16[8,2,4096]{2,1,0:T(2,128)(2,1)S(1)} async-done(((bf16[8,2,4096]{2,1,0:T(2,128)(2,1)}), bf16[8,2,4096]{2,1,0:T(2,128)(2,1)S(1)}, u32[]{:S(2)}, u32[]{:S(2)}) %all-to-all-start) | async-done | bytes 131104 | tf_op jit(solution)/shard_map/all_to_all | solution.py:65
  13.5 3.4 %all-to-all-start.1 = ((bf16[8,2,4096]{2,1,0:T(2,128)(2,1)}), bf16[8,2,4096]{2,1,0:T(2,128)(2,1)S(1)}, u32[]{:S(2)}, u32[]{:S(2)}) async-start(bf16[8,2,4096]{2,1,0:T(2,128)(2,1)} %reshape.181), calls=%async_computation.1 | async-start | bytes 262144 | tf_op jit(solution)/shard_map/all_to_all | solution.py:66
  17.6 4.7 %all-to-all-done.1 = bf16[8,2,4096]{2,1,0:T(2,128)(2,1)S(1)} async-done(((bf16[8,2,4096]{2,1,0:T(2,128)(2,1)}), bf16[8,2,4096]{2,1,0:T(2,128)(2,1)S(1)}, u32[]{:S(2)}, u32[]{:S(2)}) %all-to-all-start.1) | async-done | bytes 131104 | tf_op jit(solution)/shard_map/all_to_all | solution.py:66
  23.4 1.7 %gather_fusion = bf16[128,2,2,512]{3,2,1,0:T(2,128)(2,1)S(1)} fusion(bf16[2,2,512,64]{2,1,3,0:T(2,128)(2,1)S(1)} %pad_maximum_fusion.4, s32[1024]{0:T(1024)S(1)} %pad_clamp_fusion.1), kind=kCustom, calls=%fused_computation | custom fusion | bytes 1049088 | tf_op jit(solution)/shard_map/jit(_take)/gather | solution.py:71
  25.1 1.4 %fusion.22 = bf16[2,2,512,128]{2,1,0,3:T(2,128)(2,1)} fusion(bf16[128,2,2,512]{3,2,1,0:T(2,128)(2,1)S(1)} %gather_fusion, pred[128]{0:T(512)(128)(4,1)S(1)} %compare_and_fusion), kind=kLoop, calls=%fused_computation.49 | loop fusion | flops 262144 | bytes 1048704 | tf_op jit(solution)/shard_map/jit(_take)/select_n | solution.py:71
  26.5 4.9 %all-to-all-start.2 = ((bf16[2,2,512,128]{2,1,0,3:T(2,128)(2,1)}), bf16[2,2,512,128]{2,1,0,3:T(2,128)(2,1)S(1)}, u32[]{:S(2)}, u32[]{:S(2)}) async-start(bf16[2,2,512,128]{2,1,0,3:T(2,128)(2,1)} %fusion.22), calls=%async_computation.2 | async-start | bytes 1048576 | tf_op jit(solution)/shard_map/all_to_all | solution.py:72
  32.6 13.1 %all-to-all-done.2 = bf16[2,2,512,128]{2,1,0,3:T(2,128)(2,1)S(1)} async-done(((bf16[2,2,512,128]{2,1,0,3:T(2,128)(2,1)}), bf16[2,2,512,128]{2,1,0,3:T(2,128)(2,1)S(1)}, u32[]{:S(2)}, u32[]{:S(2)}) %all-to-all-start.2) | async-done | bytes 524320 | tf_op jit(solution)/shard_map/all_to_all | solution.py:72
  46.0 1.1 %gather_fusion.1 = bf16[64,2,2,512]{3,2,1,0:T(2,128)(2,1)S(1)} fusion(bf16[2,2,512,128]{2,1,3,0:T(2,128)(2,1)S(1)} %copy.97, s32[1024]{0:T(1024)S(1)} %pad_clamp_fusion), kind=kCustom, calls=%fused_computation.1 | custom fusion | bytes 524544 | tf_op jit(solution)/shard_map/jit(_take)/gather | solution.py:73
  53.0 1.4 %fusion.12 = f32[4,16,64,32]{2,3,1,0:T(8,128)S(1)} fusion(f32[4,16,32,64]{3,1,2,0:T(8,128)S(1)} %get-tuple-element.4), kind=kOutput, calls=%fused_computation.25 | convolution fusion | flops 50345984 | bytes 1048576 | tf_op jit(solution)/shard_map/qb,skbe->sqke/dot_general | solution.py:49
  54.4 1.4 %fusion.16 = f32[4,16,64,32]{2,3,1,0:T(8,128)S(1)} fusion(f32[4,16,32,64]{3,1,2,0:T(8,128)S(1)} %get-tuple-element.5), kind=kOutput, calls=%fused_computation.29 | convolution fusion | flops 50345984 | bytes 1048576 | tf_op jit(solution)/shard_map/qb,skbe->sqke/dot_general | solution.py:46
  55.8 1.4 %fusion.1 = f32[4,32,16,64]{3,1,2,0:T(8,128)S(1)} fusion(f32[4,16,64,32]{2,3,1,0:T(8,128)S(1)} %fusion.16, f32[4,16,32,64]{3,1,2,0:T(8,128)S(1)} %get-tuple-element.4), kind=kOutput, calls=%fused_computation.5 | convolution fusion | flops 50478080 | bytes 1572864 | tf_op jit(solution)/shard_map/qb,skbe->sqke/dot_general | solution.py:46
  57.2 1.0 %copy-done.1 = f32[4,32,16,64]{3,1,2,0:T(8,128)} copy-done((f32[4,32,16,64]{3,1,2,0:T(8,128)}, f32[4,32,16,64]{3,1,2,0:T(8,128)S(1)}, u32[]{:S(2)}) %copy-start.1) | copy-done | bytes 524312
  58.2 1.4 %fusion = f32[4,32,16,64]{3,1,2,0:T(8,128)S(1)} fusion(f32[4,16,64,32]{2,3,1,0:T(8,128)S(1)} %fusion.12, f32[4,16,32,64]{3,1,2,0:T(8,128)S(1)} %get-tuple-element.5), kind=kOutput, calls=%fused_computation.3 | convolution fusion | flops 50478080 | bytes 1572864 | tf_op jit(solution)/shard_map/qb,skbe->sqke/dot_general | solution.py:49
  59.6 1.0 %copy-done.2 = f32[4,32,16,64]{3,1,2,0:T(8,128)} copy-done((f32[4,32,16,64]{3,1,2,0:T(8,128)}, f32[4,32,16,64]{3,1,2,0:T(8,128)S(1)}, u32[]{:S(2)}) %copy-start.2) | copy-done | bytes 524312
  67.5 0.9 fusion.7
  68.4 1.1 %multiply_subtract_fusion.1 = (f32[2,16,32,64]{3,1,2,0:T(8,128)S(1)}, f32[2,16,32,64]{3,1,2,0:T(8,128)S(1)}) fusion(f32[2,16,32,64]{3,1,2,0:T(8,128)S(1)} %fusion.7, f32[16,32]{0,1:T(8,128)S(1)} %get-tuple-element.19, f32[16,32]{0,1:T(8,128)S(1)} %fusion.98, f32[2,32,64,16]{2,3,1,0:T(8,128)S(1)} %fusion.29, f32[2,16,32,64]{3,2,1,0:T(8,128)S(1)} %get-tuple-element.6), kind=kOutput, calls=%fused_computation.47 | convolution fusion | flops 13045248 | bytes 1314816 | tf_op jit(solution)/shard_map/ka,sabe->skbe/dot_general | solution.py:39
  74.1 3.4 %all-to-all-start.3 = ((bf16[8,2,4096]{2,1,0:T(2,128)(2,1)}), bf16[8,2,4096]{2,1,0:T(2,128)(2,1)S(1)}, u32[]{:S(2)}, u32[]{:S(2)}) async-start(bf16[8,2,4096]{2,1,0:T(2,128)(2,1)} %reshape.185), calls=%async_computation.3 | async-start | bytes 262144 | tf_op jit(solution)/shard_map/all_to_all | solution.py:87
  78.5 4.4 %all-to-all-done.3 = bf16[8,2,4096]{2,1,0:T(2,128)(2,1)S(1)} async-done(((bf16[8,2,4096]{2,1,0:T(2,128)(2,1)}), bf16[8,2,4096]{2,1,0:T(2,128)(2,1)S(1)}, u32[]{:S(2)}, u32[]{:S(2)}) %all-to-all-start.3) | async-done | bytes 131104 | tf_op jit(solution)/shard_map/all_to_all | solution.py:87
  83.0 3.4 %all-to-all-start.4 = ((bf16[8,2,4096]{2,1,0:T(2,128)(2,1)}), bf16[8,2,4096]{2,1,0:T(2,128)(2,1)S(1)}, u32[]{:S(2)}, u32[]{:S(2)}) async-start(bf16[8,2,4096]{2,1,0:T(2,128)(2,1)} %reshape.187), calls=%async_computation.4 | async-start | bytes 262144 | tf_op jit(solution)/shard_map/all_to_all | solution.py:89
  87.6 4.2 %all-to-all-done.4 = bf16[8,2,4096]{2,1,0:T(2,128)(2,1)S(1)} async-done(((bf16[8,2,4096]{2,1,0:T(2,128)(2,1)}), bf16[8,2,4096]{2,1,0:T(2,128)(2,1)S(1)}, u32[]{:S(2)}, u32[]{:S(2)}) %all-to-all-start.4) | async-done | bytes 131104 | tf_op jit(solution)/shard_map/all_to_all | solution.py:89
  (83 shorter events, 24.5 us)
Async XLA Ops:
  0.6 7.3 %copy-start = (s32[1,8,4,32]{3,2,1,0:T(4,128)S(1)}, s32[1,8,4,32]{3,2,1,0:T(4,128)}, u32[]{:S(2)}) copy-start(s32[1,8,4,32]{3,2,1,0:T(4,128)} %param.6) | copy-start | bytes 12292
  2.6 5.5 %copy-start.3 = (bf16[2,64,512]{2,1,0:T(8,128)(2,1)S(1)}, bf16[2,64,512]{2,1,0:T(8,128)(2,1)}, u32[]{:S(2)}) copy-start(bf16[2,64,512]{2,1,0:T(8,128)(2,1)} %param.5) | copy-start | bytes 393220
  2.6 10.8 %all-to-all-start = ((bf16[8,2,4096]{2,1,0:T(2,128)(2,1)}), bf16[8,2,4096]{2,1,0:T(2,128)(2,1)S(1)}, u32[]{:S(2)}, u32[]{:S(2)}) async-start(bf16[8,2,4096]{2,1,0:T(2,128)(2,1)} %reshape.183), calls=%async_computation | async-start | bytes 262144 | tf_op jit(solution)/shard_map/all_to_all | solution.py:65
  13.5 8.8 %all-to-all-start.1 = ((bf16[8,2,4096]{2,1,0:T(2,128)(2,1)}), bf16[8,2,4096]{2,1,0:T(2,128)(2,1)S(1)}, u32[]{:S(2)}, u32[]{:S(2)}) async-start(bf16[8,2,4096]{2,1,0:T(2,128)(2,1)} %reshape.181), calls=%async_computation.1 | async-start | bytes 262144 | tf_op jit(solution)/shard_map/all_to_all | solution.py:66
  26.5 19.2 %all-to-all-start.2 = ((bf16[2,2,512,128]{2,1,0,3:T(2,128)(2,1)}), bf16[2,2,512,128]{2,1,0,3:T(2,128)(2,1)S(1)}, u32[]{:S(2)}, u32[]{:S(2)}) async-start(bf16[2,2,512,128]{2,1,0,3:T(2,128)(2,1)} %fusion.22), calls=%async_computation.2 | async-start | bytes 1048576 | tf_op jit(solution)/shard_map/all_to_all | solution.py:72
  57.2 1.0 %copy-start.1 = (f32[4,32,16,64]{3,1,2,0:T(8,128)}, f32[4,32,16,64]{3,1,2,0:T(8,128)S(1)}, u32[]{:S(2)}) copy-start(f32[4,32,16,64]{3,1,2,0:T(8,128)S(1)} %fusion.1) | copy-start | bytes 1572868
  59.6 1.0 %copy-start.2 = (f32[4,32,16,64]{3,1,2,0:T(8,128)}, f32[4,32,16,64]{3,1,2,0:T(8,128)S(1)}, u32[]{:S(2)}) copy-start(f32[4,32,16,64]{3,1,2,0:T(8,128)S(1)} %fusion) | copy-start | bytes 1572868
  60.6 1.0 %slice-start = ((f32[4,32,16,64]{3,1,2,0:T(8,128)}), f32[2,32,16,64]{3,1,2,0:T(8,128)S(1)}, s32[]{:S(2)}) async-start(f32[4,32,16,64]{3,1,2,0:T(8,128)} %copy-done.1), calls=%async_computation.5 | async-start | bytes 1048576 | tf_op jit(solution)/shard_map/slice | solution.py:76
  62.9 1.0 %slice-start.1 = ((f32[4,32,16,64]{3,1,2,0:T(8,128)}), f32[2,32,16,64]{3,1,2,0:T(8,128)S(1)}, s32[]{:S(2)}) async-start(f32[4,32,16,64]{3,1,2,0:T(8,128)} %copy-done.2), calls=%async_computation.6 | async-start | bytes 1048576 | tf_op jit(solution)/shard_map/slice | solution.py:77
  74.1 8.8 %all-to-all-start.3 = ((bf16[8,2,4096]{2,1,0:T(2,128)(2,1)}), bf16[8,2,4096]{2,1,0:T(2,128)(2,1)S(1)}, u32[]{:S(2)}, u32[]{:S(2)}) async-start(bf16[8,2,4096]{2,1,0:T(2,128)(2,1)} %reshape.185), calls=%async_computation.3 | async-start | bytes 262144 | tf_op jit(solution)/shard_map/all_to_all | solution.py:87
  83.0 8.8 %all-to-all-start.4 = ((bf16[8,2,4096]{2,1,0:T(2,128)(2,1)}), bf16[8,2,4096]{2,1,0:T(2,128)(2,1)S(1)}, u32[]{:S(2)}, u32[]{:S(2)}) async-start(bf16[8,2,4096]{2,1,0:T(2,128)(2,1)} %reshape.187), calls=%async_computation.4 | async-start | bytes 262144 | tf_op jit(solution)/shard_map/all_to_all | solution.py:89
